TPU v7x, 512 devices: a whole 4x8x8 slice. The times are simulated.
512 devices in a mesh: grp: 32 (over y, z_lo, core), sub: 16 (over x, z_hi).
Axes of the slice: x: 4, y: 8, z: 8 (z_hi: 4, z_lo: 2; z = z_hi * 2 + z_lo), core: 2. Of those that a mesh axis runs over, the one named last changes fastest.
Arguments:
- spectra: bfloat16 [2, 6, 32768, 384], P(None, None, ('grp', 'sub'))
- partner_table: int32 [2, 32], replicated, may hold values from 0 to 31, as said below
Outputs:
- group_cross: float32 [2, 6, 32768, 1024], P(None, None, ('grp', 'sub'))
- partner_cross: float32 [2, 2, 6, 2097152], P(None, None, None, ('grp', 'sub'))
Inputs may be any that keep to these rules, and one draw needn't show every extreme that they name: partner_table[r, g] = g XOR m_r, where the round's mask m_r (1 to 30) is the same for all groups, and m_1 = m_0 XOR (31).
All inputs are finite; a program needn't handle non-finite values.
Results may differ from a plain program's by a relative error of at most 0.0041.
Values may be sent and summed in bfloat16 or wider, within the bound.
A program may use at most 64 MiB of HBM per device.

v0:
```python
import jax
import jax.numpy as jnp
from jax import lax
from jax.sharding import PartitionSpec as P

EPSILON = 1e-06


def swapped_2(x, axis, apart):
    return lax.ppermute(x, axis, [(i, i ^ 1 << apart) for i in range(lax.axis_size(axis))])


def whiten(spectra):
    values = spectra.astype(jnp.float32)
    power_mean = jnp.mean(values[0] * values[0] + values[1] * values[1], axis=0)
    return (values / jnp.sqrt(power_mean + EPSILON)).astype(jnp.bfloat16)


def left_pair_of(whitened):
    first = jnp.concatenate([whitened[0], whitened[1]], axis=-1)
    second = jnp.concatenate([whitened[1], -whitened[0]], axis=-1)
    return jnp.stack([first, second])


def cross_spectra(left_pair, right, scale):
    right_cols = jnp.concatenate([right[0], right[1]], axis=-1)
    return (
        jnp.einsum("pfcw,fdw->pfcd", left_pair, right_cols, preferred_element_type=jnp.float32)
        * scale
    )


def shards(spectra, partner_table):
    whitened = whiten(spectra)
    chan_dev = whitened.shape[2]
    windows = whitened.shape[3]
    scale = 1.0 / windows
    left_pair = left_pair_of(whitened)
    group_cross = cross_spectra(
        left_pair, lax.all_gather(whitened, "sub", axis=2, tiled=True), scale
    )
    group_total = lax.axis_size("grp")
    bit_count = group_total.bit_length() - 1
    own_group = lax.axis_index("grp")
    round_masks = [
        jnp.bitwise_xor(partner_table[round_num, own_group], own_group)
        for round_num in range(partner_table.shape[0])
    ]
    bit_list = list(range(bit_count))
    partners = []
    for round_num in range(partner_table.shape[0]):
        carried = whitened
        for bit_pos in bit_list:
            swapped = swapped_2(carried, "grp", bit_pos)
            carried = jnp.where(round_masks[round_num] >> bit_pos & 1 == 1, swapped, carried)
        partners.append(carried)
    results = []
    for partner_block in partners:
        block_cross = cross_spectra(left_pair, partner_block, scale)
        results.append(block_cross.reshape(2, block_cross.shape[1], chan_dev * chan_dev))
    partner_cross = jnp.stack(results)
    return (group_cross, partner_cross)


def solution(mesh):
    placed = (P(None, None, ("grp", "sub"), None), P())
    return jax.shard_map(
        shards,
        mesh=mesh,
        in_specs=placed,
        out_specs=(P(None, None, ("grp", "sub"), None), P(None, None, None, ("grp", "sub"))),
        check_vma=False,
    )
```

profile of v0, /device:TPU:1, one launch (start us, length us, event | category | flops | bytes accessed | tf_op | source)
XLA Modules:
  0.0 205.8 jit_solution(9915319461080288694)
XLA Ops:
  7.2 0.0 all-gather.2.cloned.1.call-start
  7.2 1.2 convert_element_type.6
  8.4 0.1 fusion.6
  8.5 0.0 copy-start.4
  8.6 1.0 divide_convert_fusion
  9.5 0.0 all-gather.2.cloned.1.call-update
  9.6 8.7 %collective-permute-start = (bf16[2,6,64,384]{3,2,1,0:T(8,128)(2,1)}, bf16[2,6,64,384]{3,2,1,0:T(8,128)(2,1)S(1)}, u32[]{:S(2)}, u32[]{:S(2)}) collective-permute-start(bf16[2,6,64,384]{3,2,1,0:T(8,128)(2,1)} %divide_convert_fusion), channel_id=1, source_target_pairs={{0,16},{16,0},{32,48},{48,32},{64,80},{80,64},{96,112},{112,96},{1... | collective-permute-start | bytes 1769480 | tf_op jit(solution)/shard_map/ppermute | solution.py:10
  18.3 0.6 constant_dynamic-slice_fusion.1
  20.2 0.0 collective-permute-done
  20.2 0.3 broadcast_select_fusion.5
  20.6 1.9 collective-permute-start.5
  22.5 3.4 %collective-permute-start.1 = (bf16[2,6,64,384]{3,2,1,0:T(8,128)(2,1)S(1)}, bf16[2,6,64,384]{3,2,1,0:T(8,128)(2,1)S(1)}, u32[]{:S(2)}, u32[]{:S(2)}) collective-permute-start(bf16[2,6,64,384]{3,2,1,0:T(8,128)(2,1)S(1)} %get-tuple-element.8), channel_id=1, source_target_pairs={{0,32},{16,48},{32,0},{48,16},{64,96},{80,112},{96,64},{112,80},{1... | collective-permute-start | bytes 1769480 | tf_op jit(solution)/shard_map/ppermute | solution.py:10
  25.9 14.2 %collective-permute-done.5 = bf16[2,6,64,384]{3,2,1,0:T(8,128)(2,1)S(1)} collective-permute-done((bf16[2,6,64,384]{3,2,1,0:T(8,128)(2,1)S(1)}, bf16[2,6,64,384]{3,2,1,0:T(8,128)(2,1)S(1)}, u32[]{:S(2)}, u32[]{:S(2)}) %collective-permute-start.5) | collective-permute-done | bytes 589856 | tf_op jit(solution)/shard_map/ppermute | solution.py:10
  40.0 0.1 broadcast_select_fusion.1
  40.1 1.9 collective-permute-start.6
  42.1 26.6 %collective-permute-done.1 = bf16[2,6,64,384]{3,2,1,0:T(8,128)(2,1)S(1)} collective-permute-done((bf16[2,6,64,384]{3,2,1,0:T(8,128)(2,1)S(1)}, bf16[2,6,64,384]{3,2,1,0:T(8,128)(2,1)S(1)}, u32[]{:S(2)}, u32[]{:S(2)}) %collective-permute-start.1) | collective-permute-done | bytes 589856 | tf_op jit(solution)/shard_map/ppermute | solution.py:10
  68.7 0.1 broadcast_select_fusion.6
  68.7 0.0 copy-start
  68.8 2.1 collective-permute-start.2
  70.8 0.0 collective-permute-done.6
  70.8 0.1 broadcast_select_fusion.2
  70.9 1.9 collective-permute-start.7
  72.9 0.1 slice_bitcast_fusion.7
  72.9 19.1 %collective-permute-done.2 = bf16[2,6,64,384]{3,2,1,0:T(8,128)(2,1)S(1)} collective-permute-done((bf16[2,6,64,384]{3,2,1,0:T(8,128)(2,1)S(1)}, bf16[2,6,64,384]{3,2,1,0:T(8,128)(2,1)S(1)}, u32[]{:S(2)}, u32[]{:S(2)}) %collective-permute-start.2) | collective-permute-done | bytes 589856 | tf_op jit(solution)/shard_map/ppermute | solution.py:10
  92.0 0.1 broadcast_select_fusion.7
  92.1 2.2 %collective-permute-start.3 = (bf16[2,6,64,384]{3,2,1,0:T(8,128)(2,1)S(1)}, bf16[2,6,64,384]{3,2,1,0:T(8,128)(2,1)S(1)}, u32[]{:S(2)}, u32[]{:S(2)}) collective-permute-start(bf16[2,6,64,384]{3,2,1,0:T(8,128)(2,1)S(1)} %broadcast_select_fusion.7), channel_id=1, source_target_pairs={{0,128},{16,144},{32,160},{48,176},{64,192},{80,208},{96,224},{112... | collective-permute-start | bytes 1769480 | tf_op jit(solution)/shard_map/ppermute | solution.py:10
  94.3 18.6 %collective-permute-done.7 = bf16[2,6,64,384]{3,2,1,0:T(8,128)(2,1)S(1)} collective-permute-done((bf16[2,6,64,384]{3,2,1,0:T(8,128)(2,1)S(1)}, bf16[2,6,64,384]{3,2,1,0:T(8,128)(2,1)S(1)}, u32[]{:S(2)}, u32[]{:S(2)}) %collective-permute-start.7) | collective-permute-done | bytes 589856 | tf_op jit(solution)/shard_map/ppermute | solution.py:10
  112.9 0.1 broadcast_select_fusion.3
  113.0 3.6 %collective-permute-start.8 = (bf16[2,6,64,384]{3,2,1,0:T(8,128)(2,1)S(1)}, bf16[2,6,64,384]{3,2,1,0:T(8,128)(2,1)S(1)}, u32[]{:S(2)}, u32[]{:S(2)}) collective-permute-start(bf16[2,6,64,384]{3,2,1,0:T(8,128)(2,1)S(1)} %broadcast_select_fusion.3), channel_id=1, source_target_pairs={{0,256},{16,272},{32,288},{48,304},{64,320},{80,336},{96,352},{112... | collective-permute-start | bytes 1769480 | tf_op jit(solution)/shard_map/ppermute | solution.py:10
  116.7 0.1 maximum_bitcast_fusion.4
  116.8 21.8 %collective-permute-done.3 = bf16[2,6,64,384]{3,2,1,0:T(8,128)(2,1)S(1)} collective-permute-done((bf16[2,6,64,384]{3,2,1,0:T(8,128)(2,1)S(1)}, bf16[2,6,64,384]{3,2,1,0:T(8,128)(2,1)S(1)}, u32[]{:S(2)}, u32[]{:S(2)}) %collective-permute-start.3) | collective-permute-done | bytes 589856 | tf_op jit(solution)/shard_map/ppermute | solution.py:10
  138.6 0.1 broadcast_select_fusion.8
  138.7 3.6 %collective-permute-start.4 = (bf16[2,6,64,384]{3,2,1,0:T(8,128)(2,1)S(1)}, bf16[2,6,64,384]{3,2,1,0:T(8,128)(2,1)S(1)}, u32[]{:S(2)}, u32[]{:S(2)}) collective-permute-start(bf16[2,6,64,384]{3,2,1,0:T(8,128)(2,1)S(1)} %broadcast_select_fusion.8), channel_id=1, source_target_pairs={{0,256},{16,272},{32,288},{48,304},{64,320},{80,336},{96,352},{112... | collective-permute-start | bytes 1769480 | tf_op jit(solution)/shard_map/ppermute | solution.py:10
  142.3 0.1 broadcast_select_fusion.4
  142.4 0.1 slice_bitcast_fusion.3
  142.5 0.7 fusion.3
  143.2 0.2 copy.8
  143.3 0.2 stack_reshape.7
  143.5 36.9 %collective-permute-done.4 = bf16[2,6,64,384]{3,2,1,0:T(8,128)(2,1)S(1)} collective-permute-done((bf16[2,6,64,384]{3,2,1,0:T(8,128)(2,1)S(1)}, bf16[2,6,64,384]{3,2,1,0:T(8,128)(2,1)S(1)}, u32[]{:S(2)}, u32[]{:S(2)}) %collective-permute-start.4) | collective-permute-done | bytes 589856 | tf_op jit(solution)/shard_map/ppermute | solution.py:10
  180.5 0.1 broadcast_select_fusion.9
  180.6 0.1 slice_bitcast_fusion.5
  180.6 0.7 fusion.4
  181.3 0.2 copy.7
  181.5 0.2 stack_reshape.6
  181.7 0.9 pad_maximum_fusion.1
  182.7 8.4 %slice_bitcast_fusion.1 = (bf16[6,1024,384]{2,1,0:T(8,128)(2,1)}, bf16[6,1024,384]{2,1,0:T(8,128)(2,1)}) fusion(bf16[2,6,1024,384]{3,2,1,0:T(8,128)(2,1)} %all-gather.2.cloned.1.call-done), kind=kLoop, calls=%fused_computation.5 | loop fusion | bytes 18874368 | tf_op jit(solution)/shard_map/squeeze | solution.py:26
  191.0 6.0 %multiply_bitcast_fusion = f32[2,6,64,1024]{3,2,0,1:T(8,128)S(1)} fusion(bf16[6,1024,384]{2,1,0:T(8,128)(2,1)} %get-tuple-element.7, bf16[6,1024,384]{2,1,0:T(8,128)(2,1)} %get-tuple-element.6, bf16[1,6,64,768]{3,2,0,1:T(8,128)(2,1)} %copy-done.3, bf16[1,6,64,768]{3,2,0,1:T(8,128)(2,1)} %copy-done.2), kind=kOutput, calls=%fused_computation.6 | convolution fusion | flops 1229979648 | bytes 13762560 | tf_op jit(solution)/shard_map/pfcw,fdw->pfcd/dot_general | solution.py:28
  197.1 1.9 copy.9
  (12 shorter events, 0.1 us)
Async XLA Ops:
  7.2 1.4 copy-start.1
  7.2 175.5 %all-gather.2.cloned.1.call-start = ((), (), s32[]{:S(2)}) async-start(), calls=%async_computation | async-start | bytes 10027008 | tf_op jit(solution)/shard_map/all_gather | solution.py:40
  8.5 9.8 %copy-start.4 = (s32[2,32]{1,0:T(2,128)S(1)}, s32[2,32]{1,0:T(2,128)}, u32[]{:S(2)}) copy-start(s32[2,32]{1,0:T(2,128)} %param.3) | copy-start | bytes 772
  9.6 10.7 %collective-permute-start = (bf16[2,6,64,384]{3,2,1,0:T(8,128)(2,1)}, bf16[2,6,64,384]{3,2,1,0:T(8,128)(2,1)S(1)}, u32[]{:S(2)}, u32[]{:S(2)}) collective-permute-start(bf16[2,6,64,384]{3,2,1,0:T(8,128)(2,1)} %divide_convert_fusion), channel_id=1, source_target_pairs={{0,16},{16,0},{32,48},{48,32},{64,80},{80,64},{96,112},{112,96},{1... | collective-permute-start | bytes 1769480 | tf_op jit(solution)/shard_map/ppermute | solution.py:10
  20.6 19.5 %collective-permute-start.5 = (bf16[2,6,64,384]{3,2,1,0:T(8,128)(2,1)S(1)}, bf16[2,6,64,384]{3,2,1,0:T(8,128)(2,1)S(1)}, u32[]{:S(2)}, u32[]{:S(2)}) collective-permute-start(bf16[2,6,64,384]{3,2,1,0:T(8,128)(2,1)S(1)} %get-tuple-element.9), channel_id=1, source_target_pairs={{0,32},{16,48},{32,0},{48,16},{64,96},{80,112},{96,64},{112,80},{1... | collective-permute-start | bytes 1769480 | tf_op jit(solution)/shard_map/ppermute | solution.py:10
  22.5 46.2 %collective-permute-start.1 = (bf16[2,6,64,384]{3,2,1,0:T(8,128)(2,1)S(1)}, bf16[2,6,64,384]{3,2,1,0:T(8,128)(2,1)S(1)}, u32[]{:S(2)}, u32[]{:S(2)}) collective-permute-start(bf16[2,6,64,384]{3,2,1,0:T(8,128)(2,1)S(1)} %get-tuple-element.8), channel_id=1, source_target_pairs={{0,32},{16,48},{32,0},{48,16},{64,96},{80,112},{96,64},{112,80},{1... | collective-permute-start | bytes 1769480 | tf_op jit(solution)/shard_map/ppermute | solution.py:10
  40.1 30.7 %collective-permute-start.6 = (bf16[2,6,64,384]{3,2,1,0:T(8,128)(2,1)S(1)}, bf16[2,6,64,384]{3,2,1,0:T(8,128)(2,1)S(1)}, u32[]{:S(2)}, u32[]{:S(2)}) collective-permute-start(bf16[2,6,64,384]{3,2,1,0:T(8,128)(2,1)S(1)} %broadcast_select_fusion.1), channel_id=1, source_target_pairs={{0,64},{16,80},{32,96},{48,112},{64,0},{80,16},{96,32},{112,48},{1... | collective-permute-start | bytes 1769480 | tf_op jit(solution)/shard_map/ppermute | solution.py:10
  68.7 4.1 %copy-start = (bf16[2,6,64,384]{3,2,1,0:T(8,128)(2,1)S(1)}, bf16[2,6,64,384]{3,2,1,0:T(8,128)(2,1)}, u32[]{:S(2)}) copy-start(bf16[2,6,64,384]{3,2,1,0:T(8,128)(2,1)} %divide_convert_fusion) | copy-start | bytes 1769476
  68.8 23.2 %collective-permute-start.2 = (bf16[2,6,64,384]{3,2,1,0:T(8,128)(2,1)S(1)}, bf16[2,6,64,384]{3,2,1,0:T(8,128)(2,1)S(1)}, u32[]{:S(2)}, u32[]{:S(2)}) collective-permute-start(bf16[2,6,64,384]{3,2,1,0:T(8,128)(2,1)S(1)} %broadcast_select_fusion.6), channel_id=1, source_target_pairs={{0,64},{16,80},{32,96},{48,112},{64,0},{80,16},{96,32},{112,48},{1... | collective-permute-start | bytes 1769480 | tf_op jit(solution)/shard_map/ppermute | solution.py:10
  70.9 42.0 %collective-permute-start.7 = (bf16[2,6,64,384]{3,2,1,0:T(8,128)(2,1)S(1)}, bf16[2,6,64,384]{3,2,1,0:T(8,128)(2,1)S(1)}, u32[]{:S(2)}, u32[]{:S(2)}) collective-permute-start(bf16[2,6,64,384]{3,2,1,0:T(8,128)(2,1)S(1)} %broadcast_select_fusion.2), channel_id=1, source_target_pairs={{0,128},{16,144},{32,160},{48,176},{64,192},{80,208},{96,224},{112... | collective-permute-start | bytes 1769480 | tf_op jit(solution)/shard_map/ppermute | solution.py:10
  92.1 46.5 %collective-permute-start.3 = (bf16[2,6,64,384]{3,2,1,0:T(8,128)(2,1)S(1)}, bf16[2,6,64,384]{3,2,1,0:T(8,128)(2,1)S(1)}, u32[]{:S(2)}, u32[]{:S(2)}) collective-permute-start(bf16[2,6,64,384]{3,2,1,0:T(8,128)(2,1)S(1)} %broadcast_select_fusion.7), channel_id=1, source_target_pairs={{0,128},{16,144},{32,160},{48,176},{64,192},{80,208},{96,224},{112... | collective-permute-start | bytes 1769480 | tf_op jit(solution)/shard_map/ppermute | solution.py:10
  113.0 29.3 %collective-permute-start.8 = (bf16[2,6,64,384]{3,2,1,0:T(8,128)(2,1)S(1)}, bf16[2,6,64,384]{3,2,1,0:T(8,128)(2,1)S(1)}, u32[]{:S(2)}, u32[]{:S(2)}) collective-permute-start(bf16[2,6,64,384]{3,2,1,0:T(8,128)(2,1)S(1)} %broadcast_select_fusion.3), channel_id=1, source_target_pairs={{0,256},{16,272},{32,288},{48,304},{64,320},{80,336},{96,352},{112... | collective-permute-start | bytes 1769480 | tf_op jit(solution)/shard_map/ppermute | solution.py:10
  116.8 63.8 %copy-start.2 = (bf16[1,6,64,768]{3,2,0,1:T(8,128)(2,1)}, bf16[1,6,64,768]{3,2,0,1:T(8,128)(2,1)S(1)}, u32[]{:S(2)}) copy-start(bf16[1,6,64,768]{3,2,0,1:T(8,128)(2,1)S(1)} %get-tuple-element.16) | copy-start | bytes 1769476
  116.8 63.8 %copy-start.3 = (bf16[1,6,64,768]{3,2,0,1:T(8,128)(2,1)}, bf16[1,6,64,768]{3,2,0,1:T(8,128)(2,1)S(1)}, u32[]{:S(2)}) copy-start(bf16[1,6,64,768]{3,2,0,1:T(8,128)(2,1)S(1)} %get-tuple-element.17) | copy-start | bytes 1769476
  138.7 41.8 %collective-permute-start.4 = (bf16[2,6,64,384]{3,2,1,0:T(8,128)(2,1)S(1)}, bf16[2,6,64,384]{3,2,1,0:T(8,128)(2,1)S(1)}, u32[]{:S(2)}, u32[]{:S(2)}) collective-permute-start(bf16[2,6,64,384]{3,2,1,0:T(8,128)(2,1)S(1)} %broadcast_select_fusion.8), channel_id=1, source_target_pairs={{0,256},{16,272},{32,288},{48,304},{64,320},{80,336},{96,352},{112... | collective-permute-start | bytes 1769480 | tf_op jit(solution)/shard_map/ppermute | solution.py:10
Sparse Core Ops, SparseCore 0:
  11.6 130.5 all-gather.1
where the time goes:
time: 206 us
  waiting for transfers between devices  137 us (67%)
  starting transfers between devices  29.4 us (14%)
  between operations  15.6 us (8%)
  local copies, waits for them, and re-layouts  11.9 us (6%)
  matrix products  7.36 us (4%)
  other arithmetic  4.31 us (2%)
    ppermute x9, waiting for transfers between devices, swapped_2(): lax.ppermute(x, axis, [(i, i ^ 1 << apart) for i in range(lax.axis_size(a...  137 us
    ppermute x9, starting transfers between devices, swapped_2(): lax.ppermute(x, axis, [(i, i ^ 1 << apart) for i in range(lax.axis_size(a...  29.4 us
    squeeze x3, local copies, waits for them, and re-layouts, cross_spectra(): right_cols = jnp.concatenate([right[0], right[1]], axis=-1)  8.5 us
    dot_general x3, matrix products, cross_spectra(): jnp.einsum('pfcw,fdw->pfcd', left_pair, right_cols, preferred_element_typ...  7.36 us
  transfers between devices with their start and end apart: 10, of which 6 were waited for; matrix products, arithmetic and copies ran while one was open for 2% of the time, Pallas kernels for 0%

commit v1 on v0

v1 whole, which is shorter than its diff:
```python
import functools

import jax
import jax.numpy as jnp
from jax import lax
from jax.experimental import pallas as pl
from jax.experimental.pallas import tpu as pltpu
from jax.sharding import PartitionSpec as P

EPSILON = 1e-06
MESH = pl.DeviceIdType.MESH
NX = 4
NZ = 4
Z_LOW = 2
ROWS = 16
NT = (((1,), (1,)), ((), ()))


def flipped(index, mask):
    out = index
    for bit in range(mask.bit_length()):
        if mask >> bit & 1:
            out = out + (1 - 2 * ((index // (1 << bit)) % 2)) * (1 << bit)
    return out


def both_parts(block):
    half = block.shape[1] // 2
    return [block, jnp.concatenate([-block[:, half:], block[:, :half]], axis=1)]


def cross_kernel(
    masks,
    pieces,
    spectra_ref,
    table_ref,
    group_ref,
    partner_ref,
    y,
    row,
    mid,
    col,
    part_in,
    gbuf,
    pbuf,
    to_row,
    to_col,
    to_part,
    gout,
    pout,
    row_send,
    row_recv,
    col_send,
    col_recv,
    res_send,
    res_recv,
    part_send,
    part_recv,
    out_sem,
    ready,
):
    bins, chans, depth = y.shape
    half = bins // 2
    windows = depth // 2
    wide = 2 * chans
    scale = 1.0 / windows
    rounds = range(len(masks))
    grp = lax.axis_index("grp")
    sub = lax.axis_index("sub")
    x, z = sub // NZ, sub % NZ

    def at(dx, dz):
        return (grp, ((x + dx + NX) % NX) * NZ + (z + dz + NZ) % NZ)

    z_low = (grp // Z_LOW) % 2

    def beside(sign):
        dz = jnp.where(sign > 0, z_low, z_low - 1)
        return (grp + Z_LOW * (1 - 2 * z_low), x * NZ + (z + dz + NZ) % NZ)

    over = [r for r, mask in enumerate(masks) if mask & Z_LOW][0]
    inner = masks[over] - Z_LOW
    peers = [(flipped(grp, mask), sub) for mask in masks]
    sides = [1 - z_low if r == over else (grp // (1 << (mask.bit_length() - 1))) % 2 for r, mask in enumerate(masks)]
    inner_peer = (flipped(grp, inner), sub)

    def bit_of(mask):
        return Z_LOW if mask & Z_LOW else 1 << (mask.bit_length() - 1)

    height = 2 * z + z_low
    meets = [(at(dx, 0), (x + dx) % NX < x, NX - 1 - dx) for dx in range(1, NX)]
    meets += [(at(0, 1), (z + 1) % NZ < z, NX), (at(0, -1), (z + NZ - 1) % NZ < z, NX - 1)]
    meets += [
        (beside(1), (height + 1) % (2 * NZ) < height, NX + 2),
        (beside(-1), (height + 2 * NZ - 1) % (2 * NZ) < height, NX + 1),
    ]
    meets += [
        (peer, (grp // bit_of(mask)) % 2 == 1, NX + 3 + r) for r, (peer, mask) in enumerate(zip(peers, masks))
    ]
    if inner:
        meets.append((inner_peer, (grp // bit_of(inner)) % 2 == 1, NX + 5))
    barrier = pltpu.get_barrier_semaphore()
    callers = 0
    for device, first, _ in meets:
        callers = callers + jnp.where(first, 1, 0)

        @pl.when(jnp.logical_not(first))
        def _(device=device):
            pl.semaphore_signal(barrier, inc=1, device_id=device, device_id_type=MESH)

    def await_ready(k):
        @pl.when(jnp.logical_not(meets[k][1]))
        def _():
            pl.semaphore_wait(ready.at[k], 1)

    def await_beside(way):
        @pl.when((height + 1 - 2 * way + 2 * NZ) % (2 * NZ) > height)
        def _():
            pl.semaphore_wait(ready.at[NX + 1 + way], 1)

    def await_col(way):
        @pl.when((z + 1 - 2 * way + NZ) % NZ > z)
        def _():
            pl.semaphore_wait(ready.at[NX - 1 + way], 1)

    def whiten(i, carry):
        rows = pl.ds(pl.multiple_of(i * ROWS, ROWS), ROWS)
        power = jnp.zeros((ROWS, windows), jnp.float32)
        for f in range(bins):
            real = spectra_ref[0, f, rows].astype(jnp.float32)
            imag = spectra_ref[1, f, rows].astype(jnp.float32)
            power = power + (real * real + imag * imag)
        factor = 1.0 / jnp.sqrt(power / bins + EPSILON)
        for f in range(bins):
            for part in range(2):
                value = spectra_ref[part, f, rows].astype(jnp.float32) * factor
                y[f, rows, part * windows : (part + 1) * windows] = value.astype(y.dtype)
        return carry

    lax.fori_loop(0, chans // ROWS, whiten, 0)
    pl.when(callers > 0)(lambda: pl.semaphore_wait(barrier, callers))
    for device, first, slot in meets:

        @pl.when(first)
        def _(device=device, slot=slot):
            pl.semaphore_signal(ready.at[slot], inc=1, device_id=device, device_id_type=MESH)


    def remote(src, dst, send, recv, device):
        return pltpu.make_async_remote_copy(
            src_ref=src, dst_ref=dst, send_sem=send, recv_sem=recv, device_id=device, device_id_type=MESH
        )

    def sign_of(way):
        return 1 - 2 * way

    def lower_upper(way, start=0, stop=None):
        stop = half if stop is None else stop
        return pl.ds(half * way + start, stop - start)

    def row_own(way, upper, piece):
        f = lower_upper(upper, *pieces[piece])
        return remote(
            y.at[f],
            row.at[(NX - 2) * (1 - way), f],
            row_send.at[way, upper, piece],
            row_recv.at[way, upper, piece],
            at(sign_of(way), 0),
        )

    def row_relay(way, piece):
        f = lower_upper(way, *pieces[piece])
        return remote(
            row.at[(NX - 2) * (1 - way), f],
            row.at[1, f],
            row_send.at[2, way, piece],
            row_recv.at[2, way, piece],
            at(sign_of(way), 0),
        )

    def col_copy(stage, way, piece):
        f = lower_upper(way, *pieces[piece])
        src, dst = ((y.at[f], mid.at[f]), (mid.at[f], col.at[0, f]), (col.at[0, f], col.at[1, f]))[stage]
        sign = sign_of(way)
        return remote(
            src,
            dst,
            col_send.at[stage, way, piece],
            col_recv.at[stage, way, piece],
            at(0, sign) if stage == 2 else beside(sign),
        )

    def bin_of(step):
        return step // 2 + half * (step % 2), 1 - 2 * (step % 2)

    def result_col(f, sign):
        return remote(to_col.at[f], gbuf.at[f, pl.ds(0, NX)], res_send.at[0, f], res_recv.at[0, f], at(0, -sign))

    def results_row(f):
        return [
            remote(
                to_row.at[dx - 1, f],
                gbuf.at[f, pl.ds(2 * NX + 2 * x, 2)],
                res_send.at[dx, f],
                res_recv.at[dx, f],
                at(dx, 0),
            )
            for dx in range(1, NX)
        ]

    def part_own(r, piece):
        start, stop = pieces[piece]
        size = stop - start
        if r == over:
            src, device = mid.at[pl.ds(half * (1 - z_low) + start, size)], inner_peer
        else:
            src, device = y.at[pl.ds(half * (1 - sides[r]) + start, size)], peers[r]
        dst = part_in.at[r, pl.ds(start, size)]
        if r == over and not inner:
            return pltpu.make_async_copy(src, dst, part_recv.at[r, piece])
        return remote(src, dst, part_send.at[r, piece], part_recv.at[r, piece], device)

    def part_await(r, piece):
        copy = part_own(r, piece)
        copy.wait() if r == over and not inner else copy.wait_recv()

    def part_result(r):
        return remote(
            to_part.at[r],
            pbuf.at[r, pl.ds(half * sides[r], half)],
            part_send.at[r, len(pieces)],
            part_recv.at[r, len(pieces)],
            peers[r],
        )

    def product(left, right):
        out = lax.dot_general(
            jnp.concatenate(left, axis=0) if len(left) > 1 else left[0],
            jnp.concatenate([part for block in right for part in both_parts(block)], axis=0),
            NT,
            preferred_element_type=jnp.float32,
        )
        return (out * scale).astype(jnp.bfloat16)

    ways = (jnp.where(height == 0, 0, 1), jnp.where(height == 0, 1, 0))
    await_beside(ways[0])
    col_copy(0, ways[0], 0).start()
    await_ready(0)
    await_ready(NX - 2)
    for way in range(2):
        row_own(way, way, 0).start()
    for way in range(2):
        row_own(way, 1 - way, 0).start()
    await_beside(ways[1])
    col_copy(0, ways[1], 0).start()
    await_ready(NX + 3 + 1 - over)
    for piece in range(len(pieces)):
        part_own(1 - over, piece).start()
    await_ready(NX - 3)
    for piece in range(1, len(pieces)):
        for way in ways:
            col_copy(0, way, piece).start()
        for way in range(2):
            row_own(way, way, piece).start()
    for piece in range(len(pieces)):
        for way in ways:
            col_copy(0, way, piece).wait_recv()
            col_copy(1, way, piece).start()
        if inner and piece == 0:
            await_ready(NX + 5)
        part_own(over, piece).start()
        for way in range(2):
            row_own(way, way, piece).wait_recv()
            row_relay(way, piece).start()
        for way in range(2):
            if piece > 0:
                row_own(way, 1 - way, piece).start()
        for way in ways:
            if piece == 0:
                await_col(way)
            col_copy(1, way, piece).wait_recv()
            col_copy(2, way, piece).start()

    def row_blocks(f):
        return [y[f]] + [row[dx - 1, f] for dx in range(1, NX)]

    def near(f, sign):
        blocks, other = row_blocks(f), col[0, f]
        along = product([blocks[0], other], blocks)
        for dx in range(NX):
            to_col[f, (x + dx) % NX] = along[chans:, dx * wide : (dx + 1) * wide]
        for dx in range(NX):
            gbuf[f, NX + (x + dx) % NX] = along[:chans, dx * wide : (dx + 1) * wide]
        across = product(blocks, [other])
        result_col(f, sign).start()
        for dx in range(1, NX):
            to_row[dx - 1, f, 0] = across[dx * chans : (dx + 1) * chans]
        gbuf[f, 2 * NX + 2 * x] = across[:chans]

    def near_step(n, carry):
        for piece, (start, stop) in enumerate(pieces):

            @pl.when(n == 2 * start)
            def _(piece=piece):
                for way in range(2):
                    row_own(way, 1 - way, piece).wait_recv()
                    row_relay(way, piece).wait_recv()

        near(*bin_of(n))
        return carry

    lax.fori_loop(0, bins, near_step, 0)

    def partner_step(n, carry):
        r, h = n // half, n % half
        f = half * jnp.where(r == 0, sides[0], sides[1]) + h
        own, other = y[f], part_in[r, h]
        to_part[r, h] = product([other], [own])
        pbuf[r, f] = product([own], [other])
        return carry

    def partner():
        for r in rounds:
            for piece in range(len(pieces)):
                part_await(r, piece)
        lax.fori_loop(0, len(masks) * half, partner_step, 0)
        for r in rounds:
            part_result(r).start()

    def far_step(n, carry):
        for piece, (start, stop) in enumerate(pieces):

            @pl.when(n == 2 * start)
            def _(piece=piece):
                if piece == len(pieces) - 1:
                    await_ready(NX + 3 + over)
                    partner()
                for way in range(2):
                    col_copy(2, way, piece).wait_recv()

        f, _ = bin_of(n)
        across = product(row_blocks(f), [col[1, f]])
        for dx in range(1, NX):
            to_row[dx - 1, f, 1] = across[dx * chans : (dx + 1) * chans]
        gbuf[f, 2 * NX + 2 * x + 1] = across[:chans]
        for copy in results_row(f):
            copy.start()
        return carry

    lax.fori_loop(0, bins, far_step, 0)

    for r in rounds:
        part_result(r).wait_recv()
    rows_even = lax.broadcasted_iota(jnp.int32, (chans, wide), 0) % 2 == 0
    lanes_low = lax.broadcasted_iota(jnp.int32, (chans, wide), 1) < chans
    in_order = jnp.broadcast_to(table_ref[0:1, 0:1], (chans, wide)) == masks[0]

    def woven(block):
        block = block.astype(jnp.float32)
        turned = pltpu.roll(block, chans, 1)
        upper = jnp.where(lanes_low, block, pltpu.roll(turned, chans - 1, 0))
        lower = jnp.where(lanes_low, pltpu.roll(turned, 1, 0), block)
        return jnp.where(rows_even, upper, lower)

    def weave(f, carry):
        first, second = woven(pbuf[0, f]), woven(pbuf[1, f])
        for r, block in enumerate((jnp.where(in_order, first, second), jnp.where(in_order, second, first))):
            for pair in range(chans // 2):
                pout[r, f, :, pair * wide : (pair + 1) * wide] = block[2 * pair : 2 * pair + 2]
        return carry

    lax.fori_loop(0, bins, weave, 0)
    partner_out = pltpu.make_async_copy(pout, partner_ref, out_sem.at[bins])
    partner_out.start()

    def group_out(f):
        return pltpu.make_async_copy(gout.at[:, f], group_ref.at[:, f], out_sem.at[f])

    def assemble(n, carry):
        f, sign = bin_of(n)
        for copy in results_row(f):
            copy.wait_recv()
        result_col(f, sign).wait_recv()

        def block_of(xa, za):
            turn = ((z - za) * sign + NZ) % NZ
            slot = jnp.where(
                turn == 0, NX + xa, jnp.where(turn == 1, 2 * NX + 2 * xa, jnp.where(turn == 2, 2 * NX + 2 * xa + 1, xa))
            )
            return gbuf[f, slot].astype(jnp.float32)

        for xa in range(NX):
            for za in range(0, NZ, 2):
                first, second = block_of(xa, za), block_of(xa, za + 1)
                lanes = pl.ds((xa * NZ + za) * chans, wide)
                gout[0, f, :, lanes] = jnp.concatenate([first[:, :chans], second[:, :chans]], axis=1)
                gout[1, f, :, lanes] = jnp.concatenate([first[:, chans:], second[:, chans:]], axis=1)
        group_out(f).start()
        return carry

    lax.fori_loop(0, bins, assemble, 0)


    for way in range(2):
        for piece in range(len(pieces)):
            for stage in range(3):
                col_copy(stage, way, piece).wait_send()
            for upper in range(2):
                row_own(way, upper, piece).wait_send()
            row_relay(way, piece).wait_send()
    for r in rounds:
        for piece in range(len(pieces)):
            if r != over or inner:
                part_own(r, piece).wait_send()
        part_result(r).wait_send()

    def drain(n, carry):
        f, sign = bin_of(n)
        for copy in results_row(f):
            copy.wait_send()
        result_col(f, sign).wait_send()
        group_out(f).wait()
        return carry

    lax.fori_loop(0, bins, drain, 0)
    partner_out.wait()


def cross(spectra, table, masks, call):
    _, bins, chans, windows = spectra.shape
    half = bins // 2
    depth, wide = 2 * windows, 2 * chans
    pieces = ((0, half - 1), (half - 1, half)) if half > 1 else ((0, half),)
    bf16 = jnp.bfloat16
    dma = pltpu.SemaphoreType.DMA
    return pl.pallas_call(
        functools.partial(cross_kernel, masks, pieces),
        in_specs=[pl.BlockSpec(memory_space=pltpu.VMEM)] * 2,
        out_specs=[pl.BlockSpec(memory_space=pl.ANY)] * 2,
        out_shape=[
            jax.ShapeDtypeStruct((2, bins, chans, NX * NZ * chans), jnp.float32),
            jax.ShapeDtypeStruct((2, bins, 2, chans * chans), jnp.float32),
        ],
        scratch_shapes=[
            pltpu.VMEM((bins, chans, depth), bf16),
            pltpu.VMEM((NX - 1, bins, chans, depth), bf16),
            pltpu.VMEM((bins, chans, depth), bf16),
            pltpu.VMEM((2, bins, chans, depth), bf16),
            pltpu.VMEM((2, half, chans, depth), bf16),
            pltpu.VMEM((bins, NX * NZ, chans, wide), bf16),
            pltpu.VMEM((2, bins, chans, wide), bf16),
            pltpu.VMEM((NX - 1, bins, 2, chans, wide), bf16),
            pltpu.VMEM((bins, NX, chans, wide), bf16),
            pltpu.VMEM((2, half, chans, wide), bf16),
            pltpu.VMEM((2, bins, chans, NX * NZ * chans), jnp.float32),
            pltpu.VMEM((2, bins, 2, chans * chans), jnp.float32),
            dma((3, 2, len(pieces))),
            dma((3, 2, len(pieces))),
            dma((3, 2, len(pieces))),
            dma((3, 2, len(pieces))),
            dma((NX, bins)),
            dma((NX, bins)),
            dma((2, len(pieces) + 1)),
            dma((2, len(pieces) + 1)),
            dma((bins + 1,)),
            pltpu.SemaphoreType.REGULAR((NX + 6,)),
        ],
        compiler_params=pltpu.CompilerParams(collective_id=call, has_side_effects=True),
        name="cross",
    )(spectra, table)


def shards(spectra, partner_table):
    groups = lax.axis_size("grp")
    first = partner_table[0, 0]
    low = jnp.minimum(first, groups - 1 - first)
    branches = [
        functools.partial(cross, masks=(mask, groups - 1 - mask), call=mask - 1) for mask in range(1, groups // 2)
    ]
    group_cross, partner = lax.switch(low - 1, branches, spectra, partner_table)
    return group_cross, partner.transpose(0, 2, 1, 3)


def solution(mesh):
    placed = (P(None, None, ("grp", "sub"), None), P())
    return jax.shard_map(
        shards,
        mesh=mesh,
        in_specs=placed,
        out_specs=(P(None, None, ("grp", "sub"), None), P(None, None, None, ("grp", "sub"))),
        check_vma=False,
    )
```

time: 206 us -> 67.3 us (0.33)
  the two profiles are of different devices: /device:TPU:1 before, /device:TPU:8 now
where the time goes in v1:
time: 67.3 us; the launch traced here: 67.5 us
  Pallas kernels  61.7 us (92%)
  local copies, waits for them, and re-layouts  3.6 us (5%)
  between operations  1.94 us (3%)
    pallas_call x1, Pallas kernels, cross(): pl.pallas_call(functools.partial(cross_kernel, masks, pieces), in_specs=[...  61.7 us
    unnamed x2, local copies, waits for them, and re-layouts  2.41 us

profile of v1, /device:TPU:8, one launch (start us, length us, event | category | flops | bytes accessed | tf_op | source)
XLA Modules:
  0.0 67.5 jit_solution(2076106490284646952)
XLA Ops:
  0.6 1.2 %slice.3 = s32[1,1]{1,0:T(1,128)} slice(s32[2,32]{1,0:T(2,128)} %param.18), slice={[0:1], [0:1]} | slice | bytes 8 | tf_op jit(solution)/shard_map/slice | solution.py:475
  3.1 62.0 %conditional.1 = ((f32[2,6,64,1024]{3,2,1,0:T(8,128)S(1)}, f32[2,6,2,4096]{3,2,1,0:T(2,128)S(1)})) conditional(s32[]{:T(128)} %clamp.3, (bf16[2,6,64,384]{3,2,1,0:T(8,128)(2,1)}, s32[2,32]{1,0:T(2,128)}) %tuple.53, (bf16[2,6,64,384]{3,2,1,0:T(8,128)(2,1)}, s32[2,32]{1,0:T(2,128)}) %tuple.53, ...), branch_computations={%region_0.0_spmd, %region_1.0_spmd, %region_2.0_spmd, %region_3.0_... | conditional | bytes 8 | solution.py:480
  3.3 61.7 %cross.22 = (f32[2,6,64,1024]{3,2,1,0:T(8,128)S(1)}, f32[2,6,2,4096]{3,2,1,0:T(2,128)S(1)}) custom-call(bf16[2,6,64,384]{3,2,1,0:T(8,128)(2,1)} %get-tuple-element.74.spectra_ref, s32[2,32]{1,0:T(2,128)} %get-tuple-element.75.table_ref), custom_call_target="tpu_custom_call" | custom-call | tf_op jit(solution)/shard_map/cond/branch_7_fun/cross/pallas_call | solution.py:436
  65.1 1.7 %copy.36 = f32[2,6,64,1024]{3,2,1,0:T(8,128)} copy(f32[2,6,64,1024]{3,2,1,0:T(8,128)S(1)} %get-tuple-element.128) | data formatting | bytes 6291456
  66.8 0.7 %copy.37 = f32[2,2,6,4096]{3,1,2,0:T(2,128)} copy(f32[2,2,6,4096]{3,1,2,0:T(2,128)S(1)} %bitcast.2) | data formatting | bytes 786432
